TPU v7x, 128 devices: a whole 4x4x4 slice. The times are simulated.
128 devices in a mesh: pool: 2 (over core), grp: 4 (over y), rep: 16 (over x, z).
Axes of the slice: x: 4, y: 4, z: 4, core: 2. Of those that a mesh axis runs over, the one named last changes fastest.
Arguments:
- queries: bfloat16 [512, 8192], P('pool', 'grp'), may hold values from -64 to 64
- keys: bfloat16 [16384, 512], P('rep', 'grp'), may hold values from -7 to 7
- values: bfloat16 [16384, 512], P('rep', 'grp'), may hold values from -6 to 6
- hidden_in: bfloat16 [512, 4096], P(('pool', 'grp', 'rep')), may hold values from -4 to 4
- o_weight: bfloat16 [8192, 4096], P('grp', 'rep'), may hold values from -0.125 to 0.125
- norm_gain: bfloat16 [4096], replicated, may hold values from 0.5 to 1.5
- routes: int32 [512, 8], P(('pool', 'grp', 'rep')), may hold values from 0 to 63, as said below
- route_weights: float32 [512, 8], P(('pool', 'grp', 'rep')), may hold values from 0.02 to 0.25
- w_gate: bfloat16 [64, 4096, 1536], P(('grp', 'rep'), None, 'pool'), may hold values from -0.09375 to 0.09375
- w_up: bfloat16 [64, 4096, 1536], P(('grp', 'rep'), None, 'pool'), may hold values from -0.09375 to 0.09375
- w_down: bfloat16 [64, 1536, 4096], P(('grp', 'rep'), 'pool'), may hold values from -0.15625 to 0.15625
Outputs:
- mid_rows: bfloat16 [512, 4096], P(('pool', 'grp', 'rep'))
- expert_mix: bfloat16 [512, 4096], P(('pool', 'grp', 'rep'))
Inputs may be any that keep to these rules, and one draw needn't show every extreme that they name: `routes`: each row names 8 different experts. In the rows of one device each expert is named by no row or by exactly 2 rows, and one expert, the same on every device, is named by 2 rows on every device.
All inputs are finite; a program needn't handle non-finite values.
Results may differ from a plain program's by a relative error of at most 0.027.
Values may be sent and summed in bfloat16 or wider, within the bound.
A program may use at most 128 MiB of HBM per device.

v0:
```python
import jax
import jax.numpy as jnp
from jax import lax
from jax.sharding import PartitionSpec as P

HEAD_DIM = 128


def expert_apply(rows_in, gate_w, up_w, down_w):
    gate_proj = jnp.dot(rows_in, gate_w, preferred_element_type=jnp.float32)
    upper = jnp.dot(rows_in, up_w, preferred_element_type=jnp.float32)
    activated = (jax.nn.silu(gate_proj) * upper).astype(jnp.bfloat16)
    return jnp.dot(activated, down_w, preferred_element_type=jnp.float32)


def per_device(
    queries,
    keys,
    values,
    hidden_in,
    o_weight,
    norm_gain,
    routes,
    route_weights,
    w_gate,
    w_up,
    w_down,
):
    kv_local = keys.shape[1] // HEAD_DIM
    heads_local = queries.shape[1] // HEAD_DIM
    group_size = heads_local // kv_local
    batch_rows = queries.shape[0]
    key_span = keys.shape[0]
    per_block = min(4, group_size)
    blocks = group_size // per_block
    score_scale = HEAD_DIM ** (-0.5)
    query_blocks = jnp.moveaxis(
        queries.reshape(batch_rows, kv_local, blocks, per_block, HEAD_DIM), 2, 0
    )
    key_heads = keys.reshape(key_span, kv_local, HEAD_DIM)
    value_heads = values.reshape(key_span, kv_local, HEAD_DIM)

    def local_part(query_block):
        scores = (
            jnp.einsum("rkhd,pkd->rkhp", query_block, key_heads, preferred_element_type=jnp.float32)
            * score_scale
        )
        top_score = jnp.max(scores, axis=-1)
        exp_scores = jnp.exp(scores - top_score[..., None])
        exp_total = jnp.sum(exp_scores, axis=-1)
        weighted = jnp.einsum(
            "rkhp,pkd->rkhd",
            exp_scores.astype(jnp.bfloat16),
            value_heads,
            preferred_element_type=jnp.float32,
        )
        return (top_score, exp_total, weighted)

    top_part, total_part, value_part = lax.map(local_part, query_blocks)
    rep_size = lax.axis_size("rep")
    share = batch_rows // rep_size
    rows_heads = share * heads_local

    def by_peer(part):
        part = jnp.moveaxis(part, 0, 2)
        return part.reshape((rep_size, rows_heads) + part.shape[4:])

    stats = jnp.stack([by_peer(top_part), by_peer(total_part)], axis=1)
    payload = jnp.concatenate([by_peer(value_part), stats.reshape(rep_size, -1, HEAD_DIM)], axis=1)
    payload = lax.all_to_all(payload, "rep", split_axis=0, concat_axis=0, tiled=True)
    weighted = payload[:, :rows_heads]
    stats = payload[:, rows_heads:].reshape(rep_size, 2, rows_heads)
    joint_top = jnp.max(stats[:, 0], axis=0)
    factors = jnp.exp(stats[:, 0] - joint_top)
    exp_total = jnp.sum(stats[:, 1] * factors, axis=0)
    weighted = jnp.sum(weighted * factors[..., None], axis=0)
    attention = (weighted / exp_total[:, None]).astype(jnp.bfloat16)
    attention = lax.all_gather(
        attention.reshape(share, heads_local * HEAD_DIM), "rep", axis=0, tiled=True
    )
    head_total = lax.psum_scatter(
        jnp.dot(attention, o_weight, preferred_element_type=jnp.float32),
        "grp",
        scatter_dimension=0,
        tiled=True,
    )
    attn_proj = head_total.astype(jnp.bfloat16)
    full_rows = lax.all_to_all(attn_proj, "rep", split_axis=0, concat_axis=1, tiled=True)
    mid_rows = (hidden_in.astype(jnp.float32) + full_rows.astype(jnp.float32)).astype(jnp.bfloat16)
    mid_wide = lax.optimization_barrier(mid_rows).astype(jnp.float32)
    inverse = lax.rsqrt(jnp.mean(mid_wide * mid_wide, axis=-1, keepdims=True) + 1e-06)
    normed = (mid_wide * inverse * norm_gain.astype(jnp.float32)).astype(jnp.bfloat16)
    row_dev, topk = routes.shape
    model_width = hidden_in.shape[1]
    group_count = lax.axis_size("grp")
    rep_count = lax.axis_size("rep")
    experts = group_count * rep_count
    capacity = max(2, 2 * row_dev * topk // experts)
    flat_routes = routes.reshape(-1)
    order = jnp.arange(flat_routes.shape[0], dtype=jnp.int32)
    same_before = (flat_routes[:, None] == flat_routes[None, :]) & (order[None, :] < order[:, None])
    position = jnp.sum(same_before.astype(jnp.int32), axis=1)
    slot_index = flat_routes * capacity + position
    chooser = jnp.any(
        jnp.arange(experts * capacity, dtype=jnp.int32)[:, None, None]
        == slot_index.reshape(row_dev, topk)[None, :, :],
        axis=2,
    ).astype(jnp.bfloat16)
    outgoing = jnp.dot(chooser, normed, preferred_element_type=jnp.float32).astype(jnp.bfloat16)
    arrived = lax.all_to_all(
        outgoing.reshape(experts, capacity, model_width),
        ("grp", "rep"),
        split_axis=0,
        concat_axis=0,
        tiled=True,
    )
    sources = arrived.shape[0]
    slots_here = arrived.shape[1]
    combined = expert_apply(
        lax.all_gather(arrived.reshape(-1, model_width), "pool", axis=0, tiled=True),
        w_gate[0],
        w_up[0],
        w_down[0],
    )
    served = (
        lax.psum_scatter(combined, "pool", scatter_dimension=0, tiled=True)
        .astype(jnp.bfloat16)
        .reshape(sources, slots_here, model_width)
    )
    returned = lax.all_to_all(served, ("grp", "rep"), split_axis=0, concat_axis=0, tiled=True)
    returned = returned.reshape(-1, model_width)
    picked = jnp.take(returned, slot_index, axis=0).reshape(row_dev, topk, model_width)
    expert_mix = jnp.sum(route_weights[..., None] * picked.astype(jnp.float32), axis=1).astype(
        jnp.bfloat16
    )
    return (mid_rows, expert_mix)


def solution(mesh):
    return jax.shard_map(
        per_device,
        mesh=mesh,
        in_specs=(
            P("pool", "grp"),
            P("rep", "grp"),
            P("rep", "grp"),
            P(("pool", "grp", "rep"), None),
            P("grp", "rep"),
            P(),
            P(("pool", "grp", "rep"), None),
            P(("pool", "grp", "rep"), None),
            P(("grp", "rep"), None, "pool"),
            P(("grp", "rep"), None, "pool"),
            P(("grp", "rep"), "pool", None),
        ),
        out_specs=(P(("pool", "grp", "rep"), None), P(("pool", "grp", "rep"), None)),
        check_vma=False,
    )
```

profile of v0, /device:TPU:0, one launch (start us, length us, event | category | flops | bytes accessed | tf_op | source)
XLA Modules:
  0.0 256.5 jit_solution(1512416310897008572)
XLA Ops:
  7.3 1.6 copy.23
  8.8 17.8 %while.14 = (s32[]{:T(128)}, f32[4,256,1,4]{1,3,2,0:T(4,128)S(1)}, f32[4,256,1,4]{1,3,2,0:T(4,128)S(1)}, f32[4,256,1,4,128]{4,1,3,2,0:T(8,128)}, bf16[4,256,1,4,...) while((s32[]{:T(128)}, f32[4,256,1,4]{1,3,2,0:T(4,128)S(1)}, ...), condition=%wide.region_3.4_spmd, body=%wide.region_0.3_spmd.sunk | while | flops 545257472 | bytes 14975609 | solution.py:59
  8.8 1.8 bitcast_reduce_fusion.2
  10.7 0.9 fusion.67
  11.6 1.6 fusion.68
  13.3 1.8 bitcast_reduce_fusion.2
  15.1 0.9 fusion.67
  16.0 1.7 fusion.68
  17.7 1.8 bitcast_reduce_fusion.2
  19.5 0.9 fusion.67
  20.5 1.7 fusion.68
  22.1 1.8 bitcast_reduce_fusion.2
  23.9 0.9 fusion.67
  24.9 1.7 fusion.68
  26.6 0.3 copy.26
  26.8 0.5 stack_reshape.6
  27.3 0.3 copy.27
  27.6 0.5 stack_reshape.7
  28.2 2.9 %copy.25 = f32[256,1,4,4,128]{4,3,2,0,1:T(4,128)S(1)} copy(f32[256,1,4,4,128]{4,0,3,1,2:T(8,128)} %bitcast.21) | data formatting | bytes 4194304 | tf_op jit(solution)/shard_map/transpose | solution.py:65
  31.1 0.2 pad_maximum_fusion
  31.3 37.1 %all_to_all.28 = f32[16,260,128]{2,1,0:T(8,128)S(1)} all-to-all(f32[16,260,128]{2,1,0:T(8,128)S(1)} %pad_maximum_fusion), channel_id=1, replica_groups=mesh['pool'=2,'grp'=4,'rep'=16] {'rep'}, dimensions={0} | all-to-all | bytes 4259840 | tf_op jit(solution)/shard_map/all_to_all | solution.py:70
  68.5 0.7 fusion.27
  69.4 0.7 fusion.37
  70.2 40.9 %all-gather.3.cloned.1.call-done = bf16[256,2048]{1,0:T(8,128)(2,1)} async-done(((bf16[16,2048]{1,0:T(8,128)(2,1)}), bf16[256,2048]{1,0:T(8,128)(2,1)}) %all-gather.3.cloned.1.call-update) | async-done | bytes 1048592 | tf_op jit(solution)/shard_map/all_gather | solution.py:78
  111.1 2.4 fusion.55
  113.6 0.2 convert_reduce_fusion
  113.9 19.6 %reduce-scatter.3.cloned.1.call-done = f32[64,256]{1,0:T(8,128)} async-done(((f32[256,256]{1,0:T(8,128)}), f32[64,256]{1,0:T(8,128)}) %reduce-scatter.3.cloned.1.call-update) | async-done | bytes 65552 | tf_op jit(solution)/shard_map/reduce_scatter | solution.py:81
  133.5 0.8 convert_element_type.55
  134.4 0.6 all_to_all.20
  135.0 6.9 %all-to-all-start.1 = ((bf16[16,4,256]{2,1,0:T(4,128)(2,1)}), bf16[16,4,256]{2,1,0:T(4,128)(2,1)S(1)}, u32[]{:S(2)}, u32[]{:S(2)}) async-start(bf16[16,4,256]{2,1,0:T(4,128)(2,1)} %all_to_all.20), calls=%async_computation.2 | async-start | bytes 65536 | tf_op jit(solution)/shard_map/all_to_all | solution.py:88
  142.1 7.5 %all-to-all-done.1 = bf16[16,4,256]{2,1,0:T(4,128)(2,1)S(1)} async-done(((bf16[16,4,256]{2,1,0:T(4,128)(2,1)}), bf16[16,4,256]{2,1,0:T(4,128)(2,1)S(1)}, u32[]{:S(2)}, u32[]{:S(2)}) %all-to-all-start.1) | async-done | bytes 32800 | tf_op jit(solution)/shard_map/all_to_all | solution.py:88
  149.6 0.1 fusion.38
  149.8 0.5 convolution_convert_fusion
  150.3 0.7 reshape.157
  151.0 20.0 %all_to_all.29 = bf16[64,2,4096]{2,1,0:T(2,128)(2,1)S(1)} all-to-all(bf16[64,2,4096]{2,1,0:T(2,128)(2,1)S(1)} %reshape.157), channel_id=1, replica_groups=mesh['pool'=2,'grp'=4,'rep'=16] {'grp','rep'}, dimensions={0} | all-to-all | bytes 2097152 | tf_op jit(solution)/shard_map/all_to_all | solution.py:110
  171.0 1.2 reshape.158
  172.3 0.2 reduce-scatter.5.cloned.1.call-start
  172.5 8.8 %all-gather.5.cloned.1.call-done = bf16[256,4096]{1,0:T(8,128)(2,1)} async-done(((bf16[128,4096]{1,0:T(8,128)(2,1)}), bf16[256,4096]{1,0:T(8,128)(2,1)}) %all-gather.5.cloned.1.call-update) | async-done | bytes 2097168 | tf_op jit(solution)/shard_map/all_gather | solution.py:120
  181.3 6.2 %fusion.25 = f32[256,768]{1,0:T(8,128)} fusion(bf16[256,4096]{1,0:T(8,128)(2,1)} %all-gather.5.cloned.1.call-done, bf16[1,4096,768]{2,1,0:T(8,128)(2,1)} %param.21), kind=kOutput, calls=%fused_computation.25 | convolution fusion | flops 1610612736 | bytes 9175040 | tf_op jit(solution)/shard_map/dot_general | solution.py:10
  187.5 11.3 %fusion.21 = f32[256,4096]{1,0:T(8,128)} fusion(bf16[1,768,4096]{2,1,0:T(8,128)(2,1)} %param.23, bf16[256,4096]{1,0:T(8,128)(2,1)S(1)} %copy-done.7, bf16[1,4096,768]{2,1,0:T(8,128)(2,1)} %param.22, f32[256,768]{1,0:T(8,128)} %fusion.25), kind=kOutput, calls=%fused_computation.21 | convolution fusion | flops 3222405120 | bytes 19660800 | tf_op jit(solution)/shard_map/dot_general | solution.py:13
  198.9 16.4 %reduce-scatter.5.cloned.1.call-done = f32[128,4096]{1,0:T(8,128)} async-done(((f32[256,4096]{1,0:T(8,128)}), f32[128,4096]{1,0:T(8,128)}) %reduce-scatter.5.cloned.1.call-update) | async-done | bytes 2097168 | tf_op jit(solution)/shard_map/reduce_scatter | solution.py:126
  215.2 1.7 convert_element_type.66
  217.0 1.5 reshape.159
  218.5 10.4 %all-to-all-start.3 = ((bf16[64,2,4096]{2,1,0:T(2,128)(2,1)}), bf16[64,2,4096]{2,1,0:T(2,128)(2,1)S(1)}, u32[]{:S(2)}, u32[]{:S(2)}) async-start(bf16[64,2,4096]{2,1,0:T(2,128)(2,1)} %reshape.159), calls=%async_computation.5 | async-start | bytes 2097152 | tf_op jit(solution)/shard_map/all_to_all | solution.py:130
  229.0 18.9 %all-to-all-done.3 = bf16[64,2,4096]{2,1,0:T(2,128)(2,1)S(1)} async-done(((bf16[64,2,4096]{2,1,0:T(2,128)(2,1)}), bf16[64,2,4096]{2,1,0:T(2,128)(2,1)S(1)}, u32[]{:S(2)}, u32[]{:S(2)}) %all-to-all-start.3) | async-done | bytes 1048608 | tf_op jit(solution)/shard_map/all_to_all | solution.py:130
  247.9 0.4 reshape.160
  248.4 0.7 gather_fusion
  249.1 0.9 multiply_reduce_fusion
  (58 shorter events, 1.1 us)
Async XLA Ops:
  7.2 104.0 %copy-start = (bf16[2048,256]{1,0:T(8,128)(2,1)S(1)}, bf16[2048,256]{1,0:T(8,128)(2,1)}, u32[]{:S(2)}) copy-start(bf16[2048,256]{1,0:T(8,128)(2,1)} %param.17) | copy-start | bytes 3145732
  7.2 103.9 %all-gather.3.cloned.1.call-start = ((), (), s32[]{:S(2)}) async-start(), calls=%async_computation.6 | async-start | bytes 1114112 | tf_op jit(solution)/shard_map/all_gather | solution.py:78
  8.8 2.8 %copy-start.1 = (bf16[1024,1,128]{2,0,1:T(8,128)(2,1)S(1)}, bf16[1024,1,128]{2,0,1:T(8,128)(2,1)}, u32[]{:S(2)}) copy-start(bf16[1024,1,128]{2,0,1:T(8,128)(2,1)} %get-tuple-element.156) | copy-start | bytes 786436 | tf_op jit(solution)/shard_map/while
  13.3 2.8 %copy-start.1 = (bf16[1024,1,128]{2,0,1:T(8,128)(2,1)S(1)}, bf16[1024,1,128]{2,0,1:T(8,128)(2,1)}, u32[]{:S(2)}) copy-start(bf16[1024,1,128]{2,0,1:T(8,128)(2,1)} %get-tuple-element.156) | copy-start | bytes 786436 | tf_op jit(solution)/shard_map/while
  17.7 2.8 %copy-start.1 = (bf16[1024,1,128]{2,0,1:T(8,128)(2,1)S(1)}, bf16[1024,1,128]{2,0,1:T(8,128)(2,1)}, u32[]{:S(2)}) copy-start(bf16[1024,1,128]{2,0,1:T(8,128)(2,1)} %get-tuple-element.156) | copy-start | bytes 786436 | tf_op jit(solution)/shard_map/while
  22.1 2.8 %copy-start.1 = (bf16[1024,1,128]{2,0,1:T(8,128)(2,1)S(1)}, bf16[1024,1,128]{2,0,1:T(8,128)(2,1)}, u32[]{:S(2)}) copy-start(bf16[1024,1,128]{2,0,1:T(8,128)(2,1)} %get-tuple-element.156) | copy-start | bytes 786436 | tf_op jit(solution)/shard_map/while
  31.3 82.3 %copy-start.4 = (s32[4,8]{1,0:T(4,128)S(1)}, s32[4,8]{1,0:T(4,128)}, u32[]{:S(2)}) copy-start(s32[4,8]{1,0:T(4,128)} %param.19) | copy-start | bytes 388
  31.3 110.8 %copy-start.5 = (bf16[4096]{0:T(1024)(128)(2,1)S(1)}, bf16[4096]{0:T(1024)(128)(2,1)}, u32[]{:S(2)}) copy-start(bf16[4096]{0:T(1024)(128)(2,1)} %param.18) | copy-start | bytes 24580
  68.4 81.2 %copy-start.3 = (bf16[4,4096]{1,0:T(4,128)(2,1)S(1)}, bf16[4,4096]{1,0:T(4,128)(2,1)}, u32[]{:S(2)}) copy-start(bf16[4,4096]{1,0:T(4,128)(2,1)} %param.16) | copy-start | bytes 98308
  70.2 63.4 %reduce-scatter.3.cloned.1.call-start = ((), (), s32[]{:S(2)}) async-start(), calls=%async_computation.7 | async-start | bytes 327680 | tf_op jit(solution)/shard_map/reduce_scatter | solution.py:81
  135.0 14.6 %all-to-all-start.1 = ((bf16[16,4,256]{2,1,0:T(4,128)(2,1)}), bf16[16,4,256]{2,1,0:T(4,128)(2,1)S(1)}, u32[]{:S(2)}, u32[]{:S(2)}) async-start(bf16[16,4,256]{2,1,0:T(4,128)(2,1)} %all_to_all.20), calls=%async_computation.2 | async-start | bytes 65536 | tf_op jit(solution)/shard_map/all_to_all | solution.py:88
  142.0 39.4 %all-gather.5.cloned.1.call-start = ((), (), s32[]{:S(2)}) async-start(), calls=%async_computation.8 | async-start | bytes 3145728 | tf_op jit(solution)/shard_map/all_gather | solution.py:120
  149.6 22.6 %copy-start.2 = (bf16[4,4096]{1,0:T(4,128)(2,1)}, bf16[4,4096]{1,0:T(4,128)(2,1)S(1)}, u32[]{:S(2)}) copy-start(bf16[4,4096]{1,0:T(4,128)(2,1)S(1)} %add_convert_fusion) | copy-start | bytes 98308
  172.3 43.0 %reduce-scatter.5.cloned.1.call-start = ((), (), s32[]{:S(2)}) async-start(), calls=%async_computation.9 | async-start | bytes 6291456 | tf_op jit(solution)/shard_map/reduce_scatter | solution.py:126
  181.3 6.2 %copy-start.7 = (bf16[256,4096]{1,0:T(8,128)(2,1)S(1)}, bf16[256,4096]{1,0:T(8,128)(2,1)}, u32[]{:S(2)}) copy-start(bf16[256,4096]{1,0:T(8,128)(2,1)} %all-gather.5.cloned.1.call-done) | copy-start | bytes 6291460
  217.0 32.1 %copy-start.6 = (f32[4,8]{1,0:T(4,128)S(1)}, f32[4,8]{1,0:T(4,128)}, u32[]{:S(2)}) copy-start(f32[4,8]{1,0:T(4,128)} %param.20) | copy-start | bytes 388
  218.5 29.4 %all-to-all-start.3 = ((bf16[64,2,4096]{2,1,0:T(2,128)(2,1)}), bf16[64,2,4096]{2,1,0:T(2,128)(2,1)S(1)}, u32[]{:S(2)}, u32[]{:S(2)}) async-start(bf16[64,2,4096]{2,1,0:T(2,128)(2,1)} %reshape.159), calls=%async_computation.5 | async-start | bytes 2097152 | tf_op jit(solution)/shard_map/all_to_all | solution.py:130
Sparse Core Ops, SparseCore 0:
  70.3 40.8 all-gather.2
  113.6 19.8 reduce-scatter.2
  172.4 8.9 all-gather.4
  199.0 16.1 reduce-scatter.4
where the time goes:
time: 257 us; the launch traced here: 256 us
  waiting for transfers between devices  112 us (44%)
  blocking collectives  57.1 us (22%)
  matrix products  34.3 us (13%)
  starting transfers between devices  17.7 us (7%)
  between operations  14 us (5%)
  local copies, waits for them, and re-layouts  11.9 us (5%)
  other arithmetic  9.24 us (4%)
    all_gather x1, waiting for transfers between devices, per_device(): lax.all_gather(attention.reshape(share, heads_local * HEAD_DIM), 'rep', a...  40.9 us
    all_to_all x1, blocking collectives, per_device(): lax.all_to_all(payload, 'rep', split_axis=0, concat_axis=0, tiled=True)  37.1 us
    all_to_all x1, blocking collectives, per_device(): lax.all_to_all(outgoing.reshape(experts, capacity, model_width), ('grp',...  20 us
    reduce_scatter x1, waiting for transfers between devices, per_device(): lax.psum_scatter(jnp.dot(attention, o_weight, preferred_element_type=jnp....  19.6 us
    all_to_all x1, waiting for transfers between devices, per_device(): lax.all_to_all(served, ('grp', 'rep'), split_axis=0, concat_axis=0, tiled...  18.9 us
    reduce_scatter x1, waiting for transfers between devices, per_device(): lax.psum_scatter(combined, 'pool', scatter_dimension=0, tiled=True)  16.4 us
    dot_general x1, matrix products, expert_apply(): return jnp.dot(activated, down_w, preferred_element_type=jnp.float32)  11.3 us
    all_to_all x1, starting transfers between devices, per_device(): lax.all_to_all(served, ('grp', 'rep'), split_axis=0, concat_axis=0, tiled...  10.4 us
  transfers between devices with their start and end apart: 6, of which 6 were waited for; matrix products, arithmetic and copies ran while one was open for 0% of the time, Pallas kernels for 0%

commit v1 on v0

--- a/solution.py
+++ b/solution.py
@@ -4,6 +4,13 @@
 from jax.sharding import PartitionSpec as P
 
 HEAD_DIM = 128
+
+
+def gather_over(value, name, d):
+    size = lax.axis_size(name)
+    pieces = jnp.stack([value for _ in range(size)])
+    pieces = lax.all_to_all(pieces, name, split_axis=0, concat_axis=0)
+    return jnp.concatenate(pieces, axis=d)
 
 
 def expert_apply(rows_in, gate_w, up_w, down_w):
@@ -117,10 +124,7 @@
     sources = arrived.shape[0]
     slots_here = arrived.shape[1]
     combined = expert_apply(
-        lax.all_gather(arrived.reshape(-1, model_width), "pool", axis=0, tiled=True),
-        w_gate[0],
-        w_up[0],
-        w_down[0],
+        gather_over(arrived.reshape(-1, model_width), "pool", 0), w_gate[0], w_up[0], w_down[0]
     )
     served = (
         lax.psum_scatter(combined, "pool", scatter_dimension=0, tiled=True)

time: 257 us -> 248 us (0.965)
  waiting for transfers between devices: 112 us -> 97.7 us
  blocking collectives: 57.1 us -> 62.6 us
    all_gather x1 -> x0, waiting for transfers between devices: 8.83 us -> none  [per_device(): lax.all_gather(arrived.reshape(-1, model_width), 'pool', axis=0, tiled=True)]
    reduce_scatter x1, waiting for transfers between devices: 16.4 us -> 10.7 us  [per_device(): lax.psum_scatter(combined, 'pool', scatter_dimension=0, tiled=True)]
    all_to_all x0 -> x1, blocking collectives: none -> 5.42 us  [gather_over(): pieces = lax.all_to_all(pieces, name, split_axis=0, concat_axis=0)]
  transfers between devices with their start and end apart: 6 -> 5, of which waited for: 6 -> 5; matrix products, arithmetic and copies ran while one was open for 0% -> 0% of each run, Pallas kernels for 0% -> 0%
where the time goes in v1:
time: 248 us; the launch traced here: 247 us
  waiting for transfers between devices  97.7 us (39%)
  blocking collectives  62.6 us (25%)
  matrix products  33.4 us (13%)
  starting transfers between devices  17.5 us (7%)
  between operations  14 us (6%)
  local copies, waits for them, and re-layouts  12.1 us (5%)
  other arithmetic  9.41 us (4%)
    all_gather x1, waiting for transfers between devices, per_device(): lax.all_gather(attention.reshape(share, heads_local * HEAD_DIM), 'rep', a...  40.9 us
    all_to_all x1, blocking collectives, per_device(): lax.all_to_all(payload, 'rep', split_axis=0, concat_axis=0, tiled=True)  37.1 us
    all_to_all x1, blocking collectives, per_device(): lax.all_to_all(outgoing.reshape(experts, capacity, model_width), ('grp',...  20.1 us
    reduce_scatter x1, waiting for transfers between devices, per_device(): lax.psum_scatter(jnp.dot(attention, o_weight, preferred_element_type=jnp....  19.6 us
    all_to_all x1, waiting for transfers between devices, per_device(): lax.all_to_all(served, ('grp', 'rep'), split_axis=0, concat_axis=0, tiled...  18.9 us
    dot_general x1, matrix products, expert_apply(): return jnp.dot(activated, down_w, preferred_element_type=jnp.float32)  11.3 us
    reduce_scatter x1, waiting for transfers between devices, per_device(): lax.psum_scatter(combined, 'pool', scatter_dimension=0, tiled=True)  10.7 us
    all_to_all x1, starting transfers between devices, per_device(): lax.all_to_all(served, ('grp', 'rep'), split_axis=0, concat_axis=0, tiled...  10.4 us
  transfers between devices with their start and end apart: 5, of which 5 were waited for; matrix products, arithmetic and copies ran while one was open for 0% of the time, Pallas kernels for 0%

profile of v1, /device:TPU:0, one launch (start us, length us, event | category | flops | bytes accessed | tf_op | source)
XLA Modules:
  0.0 246.7 jit_solution(13135555480227552452)
XLA Ops:
  7.3 1.6 copy.23
  8.8 17.6 %while.14 = (s32[]{:T(128)}, f32[4,256,1,4]{1,3,2,0:T(4,128)S(1)}, f32[4,256,1,4]{1,3,2,0:T(4,128)S(1)}, f32[4,256,1,4,128]{4,1,3,2,0:T(8,128)}, bf16[4,256,1,4,...) while((s32[]{:T(128)}, f32[4,256,1,4]{1,3,2,0:T(4,128)S(1)}, ...), condition=%wide.region_3.4_spmd, body=%wide.region_0.3_spmd.sunk | while | flops 545257472 | bytes 14975609 | solution.py:66
  8.8 1.8 bitcast_reduce_fusion.2
  10.6 0.9 fusion.67
  11.6 1.6 fusion.68
  13.2 1.8 bitcast_reduce_fusion.2
  15.0 0.9 fusion.67
  15.9 1.7 fusion.68
  17.6 1.8 bitcast_reduce_fusion.2
  19.4 0.9 fusion.67
  20.3 1.7 fusion.68
  22.0 1.8 bitcast_reduce_fusion.2
  23.8 0.9 fusion.67
  24.7 1.7 fusion.68
  26.4 0.3 copy.26
  26.7 0.5 stack_reshape.10
  27.2 0.3 copy.27
  27.4 0.5 stack_reshape.11
  28.0 2.9 %copy.25 = f32[256,1,4,4,128]{4,3,2,0,1:T(4,128)S(1)} copy(f32[256,1,4,4,128]{4,0,3,1,2:T(8,128)} %bitcast.21) | data formatting | bytes 4194304 | tf_op jit(solution)/shard_map/transpose | solution.py:72
  31.0 0.2 pad_maximum_fusion
  31.1 37.1 %all_to_all.33 = f32[16,260,128]{2,1,0:T(8,128)S(1)} all-to-all(f32[16,260,128]{2,1,0:T(8,128)S(1)} %pad_maximum_fusion), channel_id=1, replica_groups=mesh['pool'=2,'grp'=4,'rep'=16] {'rep'}, dimensions={0} | all-to-all | bytes 4259840 | tf_op jit(solution)/shard_map/all_to_all | solution.py:77
  68.4 0.7 fusion.27
  69.3 0.7 fusion.37
  70.1 40.9 %all-gather.2.cloned.1.call-done = bf16[256,2048]{1,0:T(8,128)(2,1)} async-done(((bf16[16,2048]{1,0:T(8,128)(2,1)}), bf16[256,2048]{1,0:T(8,128)(2,1)}) %all-gather.2.cloned.1.call-update) | async-done | bytes 1048592 | tf_op jit(solution)/shard_map/all_gather | solution.py:85
  111.0 2.4 fusion.55
  113.5 0.2 convert_reduce_fusion
  113.8 19.6 %reduce-scatter.3.cloned.1.call-done = f32[64,256]{1,0:T(8,128)} async-done(((f32[256,256]{1,0:T(8,128)}), f32[64,256]{1,0:T(8,128)}) %reduce-scatter.3.cloned.1.call-update) | async-done | bytes 65552 | tf_op jit(solution)/shard_map/reduce_scatter | solution.py:88
  133.4 0.8 convert_element_type.55
  134.2 0.6 all_to_all.23
  134.9 7.0 %all-to-all-start.1 = ((bf16[16,4,256]{2,1,0:T(4,128)(2,1)}), bf16[16,4,256]{2,1,0:T(4,128)(2,1)S(1)}, u32[]{:S(2)}, u32[]{:S(2)}) async-start(bf16[16,4,256]{2,1,0:T(4,128)(2,1)} %all_to_all.23), calls=%async_computation.2 | async-start | bytes 65536 | tf_op jit(solution)/shard_map/all_to_all | solution.py:95
  142.0 7.5 %all-to-all-done.1 = bf16[16,4,256]{2,1,0:T(4,128)(2,1)S(1)} async-done(((bf16[16,4,256]{2,1,0:T(4,128)(2,1)}), bf16[16,4,256]{2,1,0:T(4,128)(2,1)S(1)}, u32[]{:S(2)}, u32[]{:S(2)}) %all-to-all-start.1) | async-done | bytes 32800 | tf_op jit(solution)/shard_map/all_to_all | solution.py:95
  149.5 0.1 fusion.38
  149.7 0.5 convolution_convert_fusion
  150.1 0.7 reshape.157
  150.9 20.1 %all_to_all.34 = bf16[64,2,4096]{2,1,0:T(2,128)(2,1)} all-to-all(bf16[64,2,4096]{2,1,0:T(2,128)(2,1)S(1)} %reshape.157), channel_id=1, replica_groups=mesh['pool'=2,'grp'=4,'rep'=16] {'grp','rep'}, dimensions={0} | all-to-all | bytes 2097152 | tf_op jit(solution)/shard_map/all_to_all | solution.py:117
  171.0 1.5 stack_reshape.12
  172.4 0.2 pad_maximum_fusion.1
  172.6 5.4 %all_to_all.35 = bf16[2,128,4096]{2,1,0:T(8,128)(2,1)S(1)} all-to-all(bf16[2,128,4096]{2,1,0:T(8,128)(2,1)S(1)} %pad_maximum_fusion.1), channel_id=1, replica_groups=mesh['pool'=2,'grp'=4,'rep'=16] {'pool'}, dimensions={0} | all-to-all | bytes 4194304 | tf_op jit(solution)/shard_map/all_to_all | solution.py:12
  178.1 5.4 %fusion.25 = f32[256,768]{1,0:T(8,128)} fusion(bf16[256,4096]{1,0:T(8,128)(2,1)S(1)} %bitcast.142, bf16[1,4096,768]{2,1,0:T(8,128)(2,1)} %param.21), kind=kOutput, calls=%fused_computation.25 | convolution fusion | flops 1610612736 | bytes 9175040 | tf_op jit(solution)/shard_map/dot_general | solution.py:17
  183.5 11.3 %fusion.21 = f32[256,4096]{1,0:T(8,128)} fusion(bf16[1,768,4096]{2,1,0:T(8,128)(2,1)} %param.23, bf16[256,4096]{1,0:T(8,128)(2,1)S(1)} %bitcast.143, bf16[1,4096,768]{2,1,0:T(8,128)(2,1)} %param.22, f32[256,768]{1,0:T(8,128)} %fusion.25), kind=kOutput, calls=%fused_computation.21 | convolution fusion | flops 3222405120 | bytes 19660800 | tf_op jit(solution)/shard_map/dot_general | solution.py:20
  194.8 10.7 %reduce-scatter.5.cloned.1.call-done = f32[128,4096]{1,0:T(8,128)} async-done(((f32[256,4096]{1,0:T(8,128)}), f32[128,4096]{1,0:T(8,128)}) %reduce-scatter.5.cloned.1.call-update) | async-done | bytes 2097168 | tf_op jit(solution)/shard_map/reduce_scatter | solution.py:130
  205.5 1.7 convert_element_type.66
  207.2 1.5 reshape.159
  208.8 10.4 %all-to-all-start.4 = ((bf16[64,2,4096]{2,1,0:T(2,128)(2,1)}), bf16[64,2,4096]{2,1,0:T(2,128)(2,1)S(1)}, u32[]{:S(2)}, u32[]{:S(2)}) async-start(bf16[64,2,4096]{2,1,0:T(2,128)(2,1)} %reshape.159), calls=%async_computation.6 | async-start | bytes 2097152 | tf_op jit(solution)/shard_map/all_to_all | solution.py:134
  219.3 18.9 %all-to-all-done.4 = bf16[64,2,4096]{2,1,0:T(2,128)(2,1)S(1)} async-done(((bf16[64,2,4096]{2,1,0:T(2,128)(2,1)}), bf16[64,2,4096]{2,1,0:T(2,128)(2,1)S(1)}, u32[]{:S(2)}, u32[]{:S(2)}) %all-to-all-start.4) | async-done | bytes 1048608 | tf_op jit(solution)/shard_map/all_to_all | solution.py:134
  238.2 0.4 reshape.160
  238.6 0.7 gather_fusion
  239.4 0.9 multiply_reduce_fusion
  (55 shorter events, 1.1 us)
Async XLA Ops:
  7.2 103.8 %copy-start = (bf16[2048,256]{1,0:T(8,128)(2,1)S(1)}, bf16[2048,256]{1,0:T(8,128)(2,1)}, u32[]{:S(2)}) copy-start(bf16[2048,256]{1,0:T(8,128)(2,1)} %param.17) | copy-start | bytes 3145732
  7.2 103.8 %all-gather.2.cloned.1.call-start = ((), (), s32[]{:S(2)}) async-start(), calls=%async_computation.7 | async-start | bytes 1114112 | tf_op jit(solution)/shard_map/all_gather | solution.py:85
  10.6 1.0 copy-start.1
  15.0 1.0 copy-start.1
  19.4 1.0 copy-start.1
  23.8 1.0 copy-start.1
  69.1 44.3 %copy-start.4 = (s32[4,8]{1,0:T(4,128)S(1)}, s32[4,8]{1,0:T(4,128)}, u32[]{:S(2)}) copy-start(s32[4,8]{1,0:T(4,128)} %param.19) | copy-start | bytes 388
  69.1 72.9 %copy-start.5 = (bf16[4096]{0:T(1024)(128)(2,1)S(1)}, bf16[4096]{0:T(1024)(128)(2,1)}, u32[]{:S(2)}) copy-start(bf16[4096]{0:T(1024)(128)(2,1)} %param.18) | copy-start | bytes 24580
  69.1 80.4 %copy-start.3 = (bf16[4,4096]{1,0:T(4,128)(2,1)S(1)}, bf16[4,4096]{1,0:T(4,128)(2,1)}, u32[]{:S(2)}) copy-start(bf16[4,4096]{1,0:T(4,128)(2,1)} %param.16) | copy-start | bytes 98308
  70.0 63.4 %reduce-scatter.3.cloned.1.call-start = ((), (), s32[]{:S(2)}) async-start(), calls=%async_computation.8 | async-start | bytes 327680 | tf_op jit(solution)/shard_map/reduce_scatter | solution.py:88
  134.9 14.6 %all-to-all-start.1 = ((bf16[16,4,256]{2,1,0:T(4,128)(2,1)}), bf16[16,4,256]{2,1,0:T(4,128)(2,1)S(1)}, u32[]{:S(2)}, u32[]{:S(2)}) async-start(bf16[16,4,256]{2,1,0:T(4,128)(2,1)} %all_to_all.23), calls=%async_computation.2 | async-start | bytes 65536 | tf_op jit(solution)/shard_map/all_to_all | solution.py:95
  141.8 63.7 %reduce-scatter.5.cloned.1.call-start = ((), (), s32[]{:S(2)}) async-start(), calls=%async_computation.9 | async-start | bytes 6291456 | tf_op jit(solution)/shard_map/reduce_scatter | solution.py:130
  149.5 21.5 %copy-start.2 = (bf16[4,4096]{1,0:T(4,128)(2,1)}, bf16[4,4096]{1,0:T(4,128)(2,1)S(1)}, u32[]{:S(2)}) copy-start(bf16[4,4096]{1,0:T(4,128)(2,1)S(1)} %add_convert_fusion) | copy-start | bytes 98308
  208.8 29.5 %all-to-all-start.4 = ((bf16[64,2,4096]{2,1,0:T(2,128)(2,1)}), bf16[64,2,4096]{2,1,0:T(2,128)(2,1)S(1)}, u32[]{:S(2)}, u32[]{:S(2)}) async-start(bf16[64,2,4096]{2,1,0:T(2,128)(2,1)} %reshape.159), calls=%async_computation.6 | async-start | bytes 2097152 | tf_op jit(solution)/shard_map/all_to_all | solution.py:134
  219.3 20.1 %copy-start.6 = (f32[4,8]{1,0:T(4,128)S(1)}, f32[4,8]{1,0:T(4,128)}, u32[]{:S(2)}) copy-start(f32[4,8]{1,0:T(4,128)} %param.20) | copy-start | bytes 388
Sparse Core Ops, SparseCore 0:
  70.1 40.7 all-gather.1
  113.5 19.8 reduce-scatter.2
  195.0 10.5 reduce-scatter.4
